TPU v7x, 32 devices: a whole 2x2x4 slice. The times are simulated.
32 devices in a mesh: dp: 2 (over x), fsdp: 16 (over z, y, core).
Axes of the slice: x: 2, y: 2, z: 4, core: 2. Of those that a mesh axis runs over, the one named last changes fastest.
Arguments:
- tokens: bfloat16 [32, 512, 1024], P(('dp', 'fsdp')), may hold values from -6 to 6
- lengths: int32 [32], P(('dp', 'fsdp')), may hold values from 128 to 512, as said below
- time_embed: bfloat16 [32, 256], P(('dp', 'fsdp')), may hold values from -6 to 6
- cotangent: bfloat16 [32, 512, 1024], P(('dp', 'fsdp')), may hold values from -6 to 6
- time_weight: bfloat16 [256, 1024], P('fsdp'), may hold values from -0.1875 to 0.1875
- attn_gain: bfloat16 [1024], P('fsdp'), may hold values from 0.099609375 to 1.8984375
- attn_shift: bfloat16 [1024], P('fsdp'), may hold values from -3 to 3
- qkv_weight: bfloat16 [1024, 3072], P('fsdp'), may hold values from -0.1875 to 0.1875
- out_weight: bfloat16 [1024, 1024], P('fsdp'), may hold values from -0.75 to 0.75
- mlp_gain: bfloat16 [1024], P('fsdp'), may hold values from 0.099609375 to 1.8984375
- mlp_shift: bfloat16 [1024], P('fsdp'), may hold values from -3 to 3
- up_weight: bfloat16 [1024, 4096], P('fsdp'), may hold values from -0.1875 to 0.1875
- up_bias: bfloat16 [4096], P('fsdp'), may hold values from -3 to 3
- down_weight: bfloat16 [4096, 1024], P('fsdp'), may hold values from -0.09375 to 0.09375
- down_bias: bfloat16 [1024], P('fsdp'), may hold values from -3 to 3
Outputs:
- layer_out: bfloat16 [32, 512, 1024], P(('dp', 'fsdp'))
- token_grad: bfloat16 [32, 512, 1024], P(('dp', 'fsdp'))
- time_weight_grad: float32 [256, 1024], P('fsdp')
- attn_gain_grad: float32 [1024], P('fsdp')
- attn_shift_grad: float32 [1024], P('fsdp')
- qkv_weight_grad: float32 [1024, 3072], P('fsdp')
- out_weight_grad: float32 [1024, 1024], P('fsdp')
- mlp_gain_grad: float32 [1024], P('fsdp')
- mlp_shift_grad: float32 [1024], P('fsdp')
- up_weight_grad: float32 [1024, 4096], P('fsdp')
- up_bias_grad: float32 [4096], P('fsdp')
- down_weight_grad: float32 [4096, 1024], P('fsdp')
- down_bias_grad: float32 [1024], P('fsdp')
Inputs may be any that keep to these rules, and one draw needn't show every extreme that they name: `lengths`: each sequence's count of real tokens; one sequence of every draw has 512.
All inputs are finite; a program needn't handle non-finite values.
Results may differ from a plain program's by a relative error of at most 0.02.
Values may be sent and summed in bfloat16 or wider, within the bound.
No kernel may reach another device: no remote copies, remote signals or barrier semaphores. Data moves between devices by JAX's collectives and lax.ppermute only.
A program may use at most 192 MiB of HBM per device.

v0:
```python
import math
import jax
import jax.numpy as jnp
from jax import lax
from jax.sharding import PartitionSpec as P

HEADS = 16
HD = 64


def normalize(values_in):
    center = values_in - jnp.mean(values_in, axis=-1, keepdims=True)
    inverse = lax.rsqrt(jnp.mean(center * center, axis=-1, keepdims=True) + 1e-05)
    return (center * inverse, inverse)


def norm_back(grad_hat, normed, inverse):
    return inverse * (
        grad_hat
        - jnp.mean(grad_hat, axis=-1, keepdims=True)
        - normed * jnp.mean(grad_hat * normed, axis=-1, keepdims=True)
    )


def rotary_tables(length, head_size):
    half_size = head_size // 2
    frequency = jnp.exp(
        jnp.arange(half_size, dtype=jnp.float32) * (-2.0 * math.log(10000.0) / head_size)
    )
    angles = jnp.arange(length, dtype=jnp.float32)[:, None] * frequency[None, :]
    angles = jnp.concatenate([angles, angles], axis=-1)
    return (jnp.cos(angles)[:, None, :], jnp.sin(angles)[:, None, :])


def rotate(values_in, cosine_table, sine_table):
    half_size = values_in.shape[-1] // 2
    turned = jnp.concatenate([-values_in[..., half_size:], values_in[..., :half_size]], axis=-1)
    return values_in * cosine_table + turned * sine_table


def rotate_back(grad_in, cosine_table, sine_table):
    half_size = grad_in.shape[-1] // 2
    sined = grad_in * sine_table
    return grad_in * cosine_table + jnp.concatenate(
        [sined[..., half_size:], -sined[..., :half_size]], axis=-1
    )


def rows_dot(left, right):
    return lax.dot_general(
        left, right, (((0,), (0,)), ((), ())), preferred_element_type=jnp.float32
    )


def back_dot(grad_in, weight):
    return lax.dot_general(
        grad_in, weight, (((1,), (1,)), ((), ())), preferred_element_type=jnp.float32
    )


def scores_of(query_pair, key_pair, key_mask, factor):
    raw_scores = (
        jnp.einsum("bqgd,bkgd->bgqk", query_pair, key_pair, preferred_element_type=jnp.float32)
        * factor
    )
    return jnp.where(key_mask[:, None, None, :], raw_scores, -1000000000.0)


def per_device(
    tokens,
    lengths,
    time_embed,
    cotangent,
    time_weight,
    attn_gain,
    attn_shift,
    qkv_weight,
    out_weight,
    mlp_gain,
    mlp_shift,
    up_weight,
    up_bias,
    down_weight,
    down_bias,
):
    seq_count, length, features = tokens.shape
    flat_rows = seq_count * length
    pair_count = HEADS // 2
    factor = HD ** (-0.5)
    time_full, gain_one, shift_one, qkv_full, out_full = (
        lax.all_gather(time_weight, "fsdp", axis=0, tiled=True),
        lax.all_gather(attn_gain, "fsdp", axis=0, tiled=True),
        lax.all_gather(attn_shift, "fsdp", axis=0, tiled=True),
        lax.all_gather(qkv_weight, "fsdp", axis=0, tiled=True),
        lax.all_gather(out_weight, "fsdp", axis=0, tiled=True),
    )
    gain_two, shift_two, up_full, up_bias_full, down_full, down_bias_full = (
        lax.all_gather(mlp_gain, "fsdp", axis=0, tiled=True),
        lax.all_gather(mlp_shift, "fsdp", axis=0, tiled=True),
        lax.all_gather(up_weight, "fsdp", axis=0, tiled=True),
        lax.all_gather(up_bias, "fsdp", axis=0, tiled=True),
        lax.all_gather(down_weight, "fsdp", axis=0, tiled=True),
        lax.all_gather(down_bias, "fsdp", axis=0, tiled=True),
    )
    key_mask = jnp.arange(length, dtype=jnp.int32)[None, :] < lengths[:, None]
    residual = tokens.astype(jnp.float32)
    time_scale = (
        1.0 + jnp.dot(time_embed, time_full, preferred_element_type=jnp.float32)[:, None, :]
    )
    normed_one, inverse_one = normalize(residual)
    affine_one = normed_one * gain_one.astype(jnp.float32) + shift_one.astype(jnp.float32)
    attn_in = (affine_one * time_scale).astype(jnp.bfloat16).reshape(flat_rows, features)
    qkv = jnp.dot(attn_in, qkv_full, preferred_element_type=jnp.float32).reshape(
        seq_count, length, 3, HEADS, HD
    )
    cosine_table, sine_table = rotary_tables(length, HD)
    query_rows = rotate(qkv[:, :, 0], cosine_table, sine_table).astype(jnp.bfloat16)
    key_rows = rotate(qkv[:, :, 1], cosine_table, sine_table).astype(jnp.bfloat16)
    value_rows = qkv[:, :, 2].astype(jnp.bfloat16)

    def by_pairs(values_in):
        return values_in.reshape(seq_count, length, pair_count, 2, HD).transpose(2, 0, 1, 3, 4)

    def from_pairs(values_in):
        return values_in.transpose(1, 2, 0, 3, 4).reshape(seq_count, length, features)

    query_group = by_pairs(query_rows)
    key_group = by_pairs(key_rows)
    value_group = by_pairs(value_rows)

    def attend(operands):
        query_pair, key_pair, value_pair = operands
        scores = scores_of(query_pair, key_pair, key_mask, factor)
        row_max = jnp.max(scores, axis=-1, keepdims=True)
        exponent = jnp.exp(scores - row_max)
        row_total = jnp.sum(exponent, axis=-1, keepdims=True)
        attn_probs = (exponent / row_total).astype(jnp.bfloat16)
        mixed_rows = jnp.einsum(
            "bgqk,bkgd->bqgd", attn_probs, value_pair, preferred_element_type=jnp.float32
        )
        return (mixed_rows.astype(jnp.bfloat16), (row_max + jnp.log(row_total))[..., 0])

    context_group, log_totals = lax.map(attend, (query_group, key_group, value_group))
    context = from_pairs(context_group).reshape(flat_rows, features)
    hidden = residual + jnp.dot(context, out_full, preferred_element_type=jnp.float32).reshape(
        seq_count, length, features
    )
    normed_two, inverse_two = normalize(hidden)
    affine_two = normed_two * gain_two.astype(jnp.float32) + shift_two.astype(jnp.float32)
    mlp_in = (affine_two * time_scale).astype(jnp.bfloat16).reshape(flat_rows, features)
    pre_act = jnp.dot(mlp_in, up_full, preferred_element_type=jnp.float32) + up_bias_full.astype(
        jnp.float32
    )
    active = jax.nn.gelu(pre_act).astype(jnp.bfloat16)
    branch_out = jnp.dot(
        active, down_full, preferred_element_type=jnp.float32
    ) + down_bias_full.astype(jnp.float32)
    layer_out = (hidden + branch_out.reshape(seq_count, length, features)).astype(jnp.bfloat16)
    gain_two, shift_two, up_full, up_bias_full, down_full, down_bias_full = (
        lax.all_gather(mlp_gain, "fsdp", axis=0, tiled=True),
        lax.all_gather(mlp_shift, "fsdp", axis=0, tiled=True),
        lax.all_gather(up_weight, "fsdp", axis=0, tiled=True),
        lax.all_gather(up_bias, "fsdp", axis=0, tiled=True),
        lax.all_gather(down_weight, "fsdp", axis=0, tiled=True),
        lax.all_gather(down_bias, "fsdp", axis=0, tiled=True),
    )
    grad_out = cotangent.astype(jnp.float32) * key_mask[:, :, None].astype(jnp.float32)
    grad_branch = grad_out.astype(jnp.bfloat16).reshape(flat_rows, features)
    down_weight_grad = rows_dot(active, grad_branch)
    down_bias_grad = jnp.sum(grad_branch.astype(jnp.float32), axis=0)
    grad_active = back_dot(grad_branch, down_full)
    gelu_value, gelu_pull = jax.vjp(jax.nn.gelu, pre_act)
    grad_pre = gelu_pull(grad_active)[0].astype(jnp.bfloat16)
    up_bias_grad = jnp.sum(grad_pre.astype(jnp.float32), axis=0)
    up_weight_grad = rows_dot(mlp_in, grad_pre)
    grad_mlp_in = back_dot(grad_pre, up_full).reshape(seq_count, length, features)
    grad_affine_two = grad_mlp_in * time_scale
    grad_scale = jnp.sum(grad_mlp_in * affine_two, axis=1)
    mlp_gain_grad = jnp.sum(grad_affine_two * normed_two, axis=(0, 1))
    mlp_shift_grad = jnp.sum(grad_affine_two, axis=(0, 1))
    grad_hidden = grad_out + norm_back(
        grad_affine_two * gain_two.astype(jnp.float32), normed_two, inverse_two
    )
    time_full, gain_one, shift_one, qkv_full, out_full = (
        lax.all_gather(time_weight, "fsdp", axis=0, tiled=True),
        lax.all_gather(attn_gain, "fsdp", axis=0, tiled=True),
        lax.all_gather(attn_shift, "fsdp", axis=0, tiled=True),
        lax.all_gather(qkv_weight, "fsdp", axis=0, tiled=True),
        lax.all_gather(out_weight, "fsdp", axis=0, tiled=True),
    )
    grad_attn = grad_hidden.astype(jnp.bfloat16).reshape(flat_rows, features)
    out_weight_grad = rows_dot(context, grad_attn)
    grad_context = back_dot(grad_attn, out_full).astype(jnp.bfloat16)

    def attend_back(operands):
        query_pair, key_pair, value_pair, log_pair, grad_pair = operands
        scores = scores_of(query_pair, key_pair, key_mask, factor)
        probs_full = jnp.exp(scores - log_pair[..., None])
        attn_probs = probs_full.astype(jnp.bfloat16)
        grad_value = jnp.einsum(
            "bgqk,bqgd->bkgd", attn_probs, grad_pair, preferred_element_type=jnp.float32
        )
        grad_probs = jnp.einsum(
            "bqgd,bkgd->bgqk", grad_pair, value_pair, preferred_element_type=jnp.float32
        )
        grad_scores = probs_full * (
            grad_probs - jnp.sum(grad_probs * probs_full, axis=-1, keepdims=True)
        )
        grad_scores = grad_scores.astype(jnp.bfloat16)
        grad_query = (
            jnp.einsum("bgqk,bkgd->bqgd", grad_scores, key_pair, preferred_element_type=jnp.float32)
            * factor
        )
        grad_key = (
            jnp.einsum(
                "bgqk,bqgd->bkgd", grad_scores, query_pair, preferred_element_type=jnp.float32
            )
            * factor
        )
        return (grad_query, grad_key, grad_value)

    grad_query_group, grad_key_group, grad_value_group = lax.map(
        attend_back, (query_group, key_group, value_group, log_totals, by_pairs(grad_context))
    )
    head_shape = (seq_count, length, HEADS, HD)
    grad_query_raw = rotate_back(
        from_pairs(grad_query_group).reshape(head_shape), cosine_table, sine_table
    )
    grad_key_raw = rotate_back(
        from_pairs(grad_key_group).reshape(head_shape), cosine_table, sine_table
    )
    grad_value_raw = from_pairs(grad_value_group).reshape(head_shape)
    grad_qkv = (
        jnp.stack([grad_query_raw, grad_key_raw, grad_value_raw], axis=2)
        .astype(jnp.bfloat16)
        .reshape(flat_rows, 3 * features)
    )
    qkv_weight_grad = rows_dot(attn_in, grad_qkv)
    grad_attn_in = back_dot(grad_qkv, qkv_full).reshape(seq_count, length, features)
    grad_affine_one = grad_attn_in * time_scale
    grad_scale = grad_scale + jnp.sum(grad_attn_in * affine_one, axis=1)
    attn_gain_grad = jnp.sum(grad_affine_one * normed_one, axis=(0, 1))
    attn_shift_grad = jnp.sum(grad_affine_one, axis=(0, 1))
    token_grad = (
        grad_hidden
        + norm_back(grad_affine_one * gain_one.astype(jnp.float32), normed_one, inverse_one)
    ).astype(jnp.bfloat16)
    time_weight_grad = jnp.dot(
        time_embed.astype(jnp.float32).T, grad_scale, precision=lax.Precision.HIGHEST
    )
    parts_all = (
        lax.psum_scatter(
            time_weight_grad.astype(jnp.bfloat16), "fsdp", scatter_dimension=0, tiled=True
        ).astype(jnp.float32),
        lax.psum_scatter(
            attn_gain_grad.astype(jnp.bfloat16), "fsdp", scatter_dimension=0, tiled=True
        ).astype(jnp.float32),
        lax.psum_scatter(
            attn_shift_grad.astype(jnp.bfloat16), "fsdp", scatter_dimension=0, tiled=True
        ).astype(jnp.float32),
        lax.psum_scatter(
            qkv_weight_grad.astype(jnp.bfloat16), "fsdp", scatter_dimension=0, tiled=True
        ).astype(jnp.float32),
        lax.psum_scatter(
            out_weight_grad.astype(jnp.bfloat16), "fsdp", scatter_dimension=0, tiled=True
        ).astype(jnp.float32),
        lax.psum_scatter(
            mlp_gain_grad.astype(jnp.bfloat16), "fsdp", scatter_dimension=0, tiled=True
        ).astype(jnp.float32),
        lax.psum_scatter(
            mlp_shift_grad.astype(jnp.bfloat16), "fsdp", scatter_dimension=0, tiled=True
        ).astype(jnp.float32),
        lax.psum_scatter(
            up_weight_grad.astype(jnp.bfloat16), "fsdp", scatter_dimension=0, tiled=True
        ).astype(jnp.float32),
        lax.psum_scatter(
            up_bias_grad.astype(jnp.bfloat16), "fsdp", scatter_dimension=0, tiled=True
        ).astype(jnp.float32),
        lax.psum_scatter(
            down_weight_grad.astype(jnp.bfloat16), "fsdp", scatter_dimension=0, tiled=True
        ).astype(jnp.float32),
        lax.psum_scatter(
            down_bias_grad.astype(jnp.bfloat16), "fsdp", scatter_dimension=0, tiled=True
        ).astype(jnp.float32),
    )
    attn_parts = parts_all[:5]
    mlp_parts = parts_all[5:]
    summed = (
        lax.psum(attn_parts[0].astype(jnp.bfloat16), "dp").astype(jnp.float32),
        lax.psum(attn_parts[1].astype(jnp.bfloat16), "dp").astype(jnp.float32),
        lax.psum(attn_parts[2].astype(jnp.bfloat16), "dp").astype(jnp.float32),
        lax.psum(attn_parts[3].astype(jnp.bfloat16), "dp").astype(jnp.float32),
        lax.psum(attn_parts[4].astype(jnp.bfloat16), "dp").astype(jnp.float32),
        lax.psum(mlp_parts[0].astype(jnp.bfloat16), "dp").astype(jnp.float32),
        lax.psum(mlp_parts[1].astype(jnp.bfloat16), "dp").astype(jnp.float32),
        lax.psum(mlp_parts[2].astype(jnp.bfloat16), "dp").astype(jnp.float32),
        lax.psum(mlp_parts[3].astype(jnp.bfloat16), "dp").astype(jnp.float32),
        lax.psum(mlp_parts[4].astype(jnp.bfloat16), "dp").astype(jnp.float32),
        lax.psum(mlp_parts[5].astype(jnp.bfloat16), "dp").astype(jnp.float32),
    )
    return (
        layer_out,
        token_grad,
        summed[0],
        summed[1],
        summed[2],
        summed[3],
        summed[4],
        summed[5],
        summed[6],
        summed[7],
        summed[8],
        summed[9],
        summed[10],
    )


def solution(mesh):
    return jax.shard_map(
        per_device,
        mesh=mesh,
        in_specs=(
            P(("dp", "fsdp"), None, None),
            P(("dp", "fsdp")),
            P(("dp", "fsdp"), None),
            P(("dp", "fsdp"), None, None),
            P("fsdp", None),
            P("fsdp"),
            P("fsdp"),
            P("fsdp", None),
            P("fsdp", None),
            P("fsdp"),
            P("fsdp"),
            P("fsdp", None),
            P("fsdp"),
            P("fsdp", None),
            P("fsdp"),
        ),
        out_specs=(
            P(("dp", "fsdp"), None, None),
            P(("dp", "fsdp"), None, None),
            P("fsdp", None),
            P("fsdp"),
            P("fsdp"),
            P("fsdp", None),
            P("fsdp", None),
            P("fsdp"),
            P("fsdp"),
            P("fsdp", None),
            P("fsdp"),
            P("fsdp", None),
            P("fsdp"),
        ),
        check_vma=False,
    )
```

profile of v0, /device:TPU:0, one launch (start us, length us, event | category | flops | bytes accessed | tf_op | source)
XLA Modules:
  0.0 823.5 jit_solution(15790023884834420819)
XLA Ops:
  15.5 37.3 %all-reduce.12 = (bf16[1024]{0:T(1024)(128)(2,1)S(1)}, bf16[1024]{0:T(1024)(128)(2,1)S(1)}, bf16[1024]{0:T(1024)(128)(2,1)S(1)}, bf16[1024]{0:T(1024)(128)(2,1)S(1)}) all-reduce(bf16[1024]{0:T(1024)(128)(2,1)S(1)} %dynamic-update-slice.1, bf16[1024]{0:T(1024)(128)(2,1)S(1)} %dynamic-update-slice, ...), channel_id=1, replica_groups=mesh['dp'=2,'fsdp'=16] {'fsdp'}, use_global_device_ids=true, to_apply=%add.1 | all-reduce | flops 4096 | bytes 16384
  53.6 17.7 %all-gather = bf16[16,1,256]{2,1,0:T(2,128)(2,1)S(1)} all-gather(bf16[1,1,256]{2,1,0:T(2,128)(2,1)S(1)} %reshape.823), channel_id=1, replica_groups=mesh['dp'=2,'fsdp'=16] {'fsdp'}, dimensions={0}, use_global_device_ids=true | all-gather | bytes 8704 | tf_op jit(solution)/shard_map/all_gather | solution.py:101
  72.9 21.5 %all_gather.41 = bf16[256,1024]{1,0:T(8,128)(2,1)S(1)} all-gather(bf16[16,1024]{1,0:T(8,128)(2,1)S(1)} %copy-done.9), channel_id=1, replica_groups=mesh['dp'=2,'fsdp'=16] {'fsdp'}, dimensions={0}, use_global_device_ids=true | all-gather | bytes 557056 | tf_op jit(solution)/shard_map/all_gather | solution.py:91
  94.6 8.6 %copy.59 = bf16[3072,1024]{1,0:T(8,128)(2,1)} copy(bf16[3072,1024]{0,1:T(8,128)(2,1)} %bitcast.284) | data formatting | bytes 12582912 | tf_op jit(solution)/shard_map/dot_general | solution.py:113
  103.2 6.4 convolution_bitcast_fusion.1
  112.3 2.5 fusion.89
  114.8 39.9 %while.28 = (s32[]{:T(128)}, bf16[8,1,512,2,64]{2,4,3,1,0:T(8,128)(2,1)}, f32[8,1,2,512]{3,2,1,0:T(2,128)S(1)}, bf16[8,1,512,2,64]{2,4,3,1,0:T(8,128)(2,1)}, bf1...) while((s32[]{:T(128)}, ...), condition=%wide.region_5.6_spmd.clone, body=%wide.region_2.5_spmd.clone.sunk | while | flops 140574208 | bytes 6852709 | solution.py:143
  127.5 2.3 fusion.159
  152.4 2.3 fusion.159
  154.8 3.3 fusion.122
  158.4 34.5 %all-gather.10.cloned.1.call-done = bf16[1024,4096]{1,0:T(8,128)(2,1)} async-done(((bf16[64,4096]{1,0:T(8,128)(2,1)}), bf16[1024,4096]{1,0:T(8,128)(2,1)}) %all-gather.10.cloned.1.call-update) | async-done | bytes 8388624 | tf_op jit(solution)/shard_map/all_gather | solution.py:100
  193.0 10.3 %fusion.118 = f32[512,4096]{1,0:T(8,128)} fusion(bf16[1024,4096]{1,0:T(8,128)(2,1)} %all-gather.10.cloned.1.call-done, f32[1,512,1024]{2,1,0:T(8,128)S(1)} %get-tuple-element.271, f32[1024]{0:T(1024)S(1)} %convert_element_type.239, f32[1024]{0:T(1024)S(1)} %convert_element_type.238, f32[512]{0:T(512)S(1)} %add_rsqrt_fusion, ...), kind=kOutput, calls=%fused_computation.184 | convolution fusion | flops 4298113024 | bytes 18890752 | tf_op jit(solution)/shard_map/dot_general | solution.py:151
  203.3 64.6 %all-gather.12.cloned.1.call-done = bf16[4096,1024]{1,0:T(8,128)(2,1)} async-done(((bf16[256,1024]{1,0:T(8,128)(2,1)}), bf16[4096,1024]{1,0:T(8,128)(2,1)}) %all-gather.12.cloned.1.call-update) | async-done | bytes 8388624 | tf_op jit(solution)/shard_map/all_gather | solution.py:102
  267.9 13.6 %fusion.123 = (bf16[4096]{0:T(1024)(128)(2,1)S(1)}, bf16[512,4096]{1,0:T(8,128)(2,1)S(1)}) fusion(f32[512,4096]{1,0:T(8,128)} %fusion.118, f32[4096]{0:T(1024)S(1)} %bitcast.298, bf16[4096,1024]{1,0:T(8,128)(2,1)} %all-gather.12.cloned.1.call-done, f32[512]{0:T(512)S(1)} %fusion.109, bf16[1,512,1024]{2,1,0:T(8,128)(2,1)} %param.22), kind=kOutput, calls=%fused_computation.188 | convolution fusion | flops 4342673408 | bytes 22046720 | tf_op jit(solution)/shard_map/dot_general | solution.py:56
  281.5 5.2 fusion.79
  290.2 2.6 convolution_convert_fusion.4
  292.8 4.5 convolution_convert_fusion.5
  297.3 2.3 copy.67
  299.7 82.7 %while.29 = (s32[]{:T(128)}, f32[8,1,512,2,64]{2,4,3,1,0:T(8,128)}, f32[8,1,512,2,64]{2,4,3,1,0:T(8,128)}, bf16[8,1,512,2,64]{2,4,3,1,0:T(8,128)(2,1)}, bf16[8,1...) while((s32[]{:T(128)}, f32[8,1,512,2,64]{2,4,3,1,0:T(8,128)}, ...), condition=%wide.region_12.13_spmd.clone, body=%wide.region_10.12_spmd.clone.sunk | while | flops 340393472 | bytes 17459324 | solution.py:222
  382.4 2.9 broadcast_multiply_fusion.1
  392.6 6.1 convolution_convert_fusion.3
  398.7 9.2 %convolution_convert_fusion.2 = bf16[1024,4096]{1,0:T(8,128)(2,1)} fusion(bf16[512,4096]{1,0:T(8,128)(2,1)} %copy-done.14, f32[1,512,1024]{2,1,0:T(8,128)S(1)} %get-tuple-element.271, f32[1024]{0:T(1024)S(1)} %convert_element_type.239, f32[1024]{0:T(1024)S(1)} %convert_element_type.238, f32[512]{0:T(512)S(1)} %add_rsqrt_fusion, ...), kind=kOutput, calls=%fused_computation.69 | convolution fusion | flops 4302307328 | bytes 14696448 | tf_op jit(solution)/shard_map/dot_general | solution.py:50
  408.4 14.2 %convolution_convert_fusion.1 = bf16[4096,1024]{1,0:T(8,128)(2,1)} fusion(bf16[1,512,1024]{2,1,0:T(8,128)(2,1)} %param.22, f32[512]{0:T(512)S(1)} %fusion.109, f32[512,4096]{1,0:T(8,128)} %fusion.118, f32[4096]{0:T(1024)S(1)} %bitcast.299), kind=kOutput, calls=%fused_computation.68 | convolution fusion | flops 4321705984 | bytes 17844224 | tf_op jit(solution)/shard_map/dot_general | solution.py:50
  426.3 8.2 fusion.69
  436.3 59.9 %all-reduce.11 = (bf16[1024]{0:T(1024)(128)(2,1)S(1)}, bf16[1024]{0:T(1024)(128)(2,1)S(1)}, bf16[1024]{0:T(1024)(128)(2,1)S(1)}, bf16[1024]{0:T(1024)(128)(2,1)S...) all-reduce(bf16[1024]{0:T(1024)(128)(2,1)S(1)} %dynamic-update-slic, ...), channel_id=1, replica_groups=mesh['dp'=2,'fsdp'=16] {'fsdp'}, use_global_device_ids=true, to_apply=%add.4 | all-reduce | flops 10240 | bytes 40960
  497.8 4.4 fusion.68
  502.2 87.4 %reduce-scatter.12.cloned.1.call-done = bf16[64,4096]{1,0:T(8,128)(2,1)} async-done(((bf16[1024,4096]{1,0:T(8,128)(2,1)}), bf16[64,4096]{1,0:T(8,128)(2,1)}) %reduce-scatter.12.cloned.1.call-update) | async-done | bytes 524304 | tf_op jit(solution)/shard_map/reduce_scatter | solution.py:273
  589.6 107.2 %reduce-scatter.14.cloned.1.call-done = bf16[256,1024]{1,0:T(8,128)(2,1)} async-done(((bf16[4096,1024]{1,0:T(8,128)(2,1)}), bf16[256,1024]{1,0:T(8,128)(2,1)}) %reduce-scatter.14.cloned.1.call-update) | async-done | bytes 524304 | tf_op jit(solution)/shard_map/reduce_scatter | solution.py:279
  696.8 12.2 %fusion.84 = bf16[1,512,1024]{2,1,0:T(8,128)(2,1)} fusion(f32[1,512,1024]{2,1,0:T(8,128)S(1)} %get-tuple-element.271, bf16[4096,1024]{1,0:T(8,128)(2,1)} %all-gather.12.cloned.1.call-done, f32[1024]{0:T(1024)S(1)} %convert_element_type.243, f32[512,4096]{1,0:T(8,128)} %fusion.118, f32[4096]{0:T(1024)S(1)} %bitcast.300), kind=kOutput, calls=%fused_computation.120 | convolution fusion | flops 4317511680 | bytes 19943424 | tf_op jit(solution)/shard_map/dot_general | solution.py:155
  709.0 47.7 %reduce-scatter.6.cloned.1.call-done = bf16[16,1024]{1,0:T(8,128)(2,1)} async-done(((bf16[256,1024]{1,0:T(8,128)(2,1)}), bf16[16,1024]{1,0:T(8,128)(2,1)}) %reduce-scatter.6.cloned.1.call-update) | async-done | bytes 32784 | tf_op jit(solution)/shard_map/reduce_scatter | solution.py:252
  756.7 9.3 %all-reduce.13 = (bf16[16,1024]{1,0:T(8,128)(2,1)S(1)}, bf16[64]{0:T(256)(128)(2,1)S(1)}, bf16[64]{0:T(256)(128)(2,1)S(1)}, bf16[64]{0:T(256)(128)(2,1)S(1)}, bf...) all-reduce(bf16[16,1024]{1,0:T(8,128)(2,1)} %reduce-scatter.6.clone, ...), channel_id=1, replica_groups=mesh['dp'=2,'fsdp'=16] {'dp'}, use_global_device_ids=true, to_apply=%region_18.19 | all-reduce | flops 16960 | bytes 67840 | tf_op jit(solution)/shard_map/psum | solution.py:289
  769.8 39.9 %all-reduce.17.cloned.1.call-done = (bf16[64,3072]{1,0:T(8,128)(2,1)}, bf16[64,1024]{1,0:T(8,128)(2,1)}, bf16[64,4096]{1,0:T(8,128)(2,1)}, bf16[256,1024]{1,0:T(8,128)(2,1)}) async-done(((bf16[64,3072]{1,0:T(8,128)(2,1)}, bf16[64,1024]{1,0:T(8,128)(2,1)}, bf16[64,4096]{1,0:T(8,128)(2,1)}, bf16[256,1024]{1,0:T(8,128)(2,1)}), (bf16[64,3072]{1,0:T(8,128)(2,1)}, bf16[64,1024]{1,0:T(8,128)(2,1)}, ...) | async-done | bytes 1572880 | tf_op jit(solution)/shard_map/psum | solution.py:292
  (229 shorter events, 157.4 us)
Async XLA Ops:
  7.2 65.0 %copy-start.2 = (bf16[1,512,1024]{2,1,0:T(8,128)(2,1)S(1)}, bf16[1,512,1024]{2,1,0:T(8,128)(2,1)}, u32[]{:S(2)}) copy-start(bf16[1,512,1024]{2,1,0:T(8,128)(2,1)} %param.19) | copy-start | bytes 3145732
  7.2 65.7 %copy-start.9 = (bf16[16,1024]{1,0:T(8,128)(2,1)S(1)}, bf16[16,1024]{1,0:T(8,128)(2,1)}, u32[]{:S(2)}) copy-start(bf16[16,1024]{1,0:T(8,128)(2,1)} %param.23) | copy-start | bytes 98308
  7.2 87.4 %all-gather.6.cloned.1.call-start = ((), (), s32[]{:S(2)}) async-start(), calls=%async_computation.5 | async-start | bytes 6684672 | tf_op jit(solution)/shard_map/all_gather | solution.py:94
  7.9 146.9 %all-gather.8.cloned.1.call-start = ((), (), s32[]{:S(2)}) async-start(), calls=%async_computation.6 | async-start | bytes 2228224 | tf_op jit(solution)/shard_map/all_gather | solution.py:95
  8.7 85.7 %copy-start.10 = (bf16[1,256]{1,0:T(2,128)(2,1)S(1)}, bf16[1,256]{1,0:T(2,128)(2,1)}, u32[]{:S(2)}) copy-start(bf16[1,256]{1,0:T(2,128)(2,1)} %param.21) | copy-start | bytes 1540
  8.7 184.3 %all-gather.10.cloned.1.call-start = ((), (), s32[]{:S(2)}) async-start(), calls=%async_computation.7 | async-start | bytes 8912896 | tf_op jit(solution)/shard_map/all_gather | solution.py:100
  9.4 258.5 %all-gather.12.cloned.1.call-start = ((), (), s32[]{:S(2)}) async-start(), calls=%async_computation.8 | async-start | bytes 8912896 | tf_op jit(solution)/shard_map/all_gather | solution.py:102
  10.0 492.2 %reduce-scatter.10.cloned.1.call-start = ((), (), s32[]{:S(2)}) async-start(), calls=%async_computation.11 | async-start | bytes 2228224 | tf_op jit(solution)/shard_map/reduce_scatter | solution.py:264
  267.9 13.7 %copy-start.12 = (bf16[1024,4096]{1,0:T(8,128)(2,1)S(1)}, bf16[1024,4096]{1,0:T(8,128)(2,1)}, u32[]{:S(2)}) copy-start(bf16[1024,4096]{1,0:T(8,128)(2,1)} %all-gather.10.cloned.1.call-done) | copy-start | bytes 25165828
  281.5 5.2 copy-start.14
  286.8 1.2 copy-start.5
  288.0 2.2 copy-start.6
  288.9 1.3 copy-start.4
  299.6 202.6 %reduce-scatter.8.cloned.1.call-start = ((), (), s32[]{:S(2)}) async-start(), calls=%async_computation.10 | async-start | bytes 6684672 | tf_op jit(solution)/shard_map/reduce_scatter | solution.py:261
  385.9 1.6 copy-start
  385.9 2.2 copy-start.1
  389.3 1.2 copy-start.7
  398.7 190.9 %reduce-scatter.12.cloned.1.call-start = ((), (), s32[]{:S(2)}) async-start(), calls=%async_computation.12 | async-start | bytes 8912896 | tf_op jit(solution)/shard_map/reduce_scatter | solution.py:273
  408.0 288.8 %reduce-scatter.14.cloned.1.call-start = ((), (), s32[]{:S(2)}) async-start(), calls=%async_computation.13 | async-start | bytes 8912896 | tf_op jit(solution)/shard_map/reduce_scatter | solution.py:279
  422.6 0.7 copy-start.11
  422.6 2.0 copy-start.13
  422.6 334.1 %reduce-scatter.6.cloned.1.call-start = ((), (), s32[]{:S(2)}) async-start(), calls=%async_computation.9 | async-start | bytes 557056 | tf_op jit(solution)/shard_map/reduce_scatter | solution.py:252
  434.6 1.4 copy-start.3
  497.5 312.2 %all-reduce.17.cloned.1.call-start = ((), (), s32[]{:S(2)}) async-start(), calls=%async_computation.14 | async-start | bytes 3145728 | tf_op jit(solution)/shard_map/psum | solution.py:292
  809.7 5.7 copy-start.8
Sparse Core Ops, SparseCore 0:
  10.3 64.5 all-gather.5
  77.0 40.6 all-gather.7
  119.9 73.0 all-gather.9
  195.0 72.8 all-gather.11
  299.7 60.4 reduce-scatter.9
  398.8 84.3 reduce-scatter.7
  487.3 102.2 reduce-scatter.11
  593.6 103.0 reduce-scatter.13
  700.9 55.8 reduce-scatter.5
  759.1 50.5 all-reduce.16
where the time goes:
time: 828 us; the launch traced here: 824 us
  waiting for transfers between devices  384 us (46%)
  matrix products  199 us (24%)
  blocking collectives  146 us (18%)
  other arithmetic  51.4 us (6%)
  local copies, waits for them, and re-layouts  24.6 us (3%)
  between operations  17.4 us (2%)
    reduce_scatter x1, waiting for transfers between devices, per_device(): lax.psum_scatter(down_weight_grad.astype(jnp.bfloat16), 'fsdp', scatter_d...  107 us
    unnamed x2, blocking collectives  97.2 us
    reduce_scatter x1, waiting for transfers between devices, per_device(): lax.psum_scatter(up_weight_grad.astype(jnp.bfloat16), 'fsdp', scatter_dim...  87.4 us
    all_gather x1, waiting for transfers between devices, per_device(): lax.all_gather(down_weight, 'fsdp', axis=0, tiled=True)  64.6 us
    reduce_scatter x1, waiting for transfers between devices, per_device(): lax.psum_scatter(time_weight_grad.astype(jnp.bfloat16), 'fsdp', scatter_d...  47.7 us
    psum x1, waiting for transfers between devices, per_device(): lax.psum(attn_parts[3].astype(jnp.bfloat16), 'dp').astype(jnp.float32)  39.9 us
    all_gather x1, waiting for transfers between devices, per_device(): lax.all_gather(up_weight, 'fsdp', axis=0, tiled=True)  34.5 us
    dot_general x4, matrix products, rows_dot(): lax.dot_general(left, right, (((0,), (0,)), ((), ())), preferred_element_...  32 us
  transfers between devices with their start and end apart: 10, of which 6 were waited for; matrix products, arithmetic and copies ran while one was open for 28% of the time, Pallas kernels for 0%

commit v1 on v0

--- a/solution.py
+++ b/solution.py
@@ -289,7 +289,9 @@
         lax.psum(attn_parts[0].astype(jnp.bfloat16), "dp").astype(jnp.float32),
         lax.psum(attn_parts[1].astype(jnp.bfloat16), "dp").astype(jnp.float32),
         lax.psum(attn_parts[2].astype(jnp.bfloat16), "dp").astype(jnp.float32),
-        lax.psum(attn_parts[3].astype(jnp.bfloat16), "dp").astype(jnp.float32),
+        jnp.sum(lax.all_gather(attn_parts[3].astype(jnp.bfloat16), "dp"), axis=0).astype(
+            jnp.float32
+        ),
         lax.psum(attn_parts[4].astype(jnp.bfloat16), "dp").astype(jnp.float32),
         lax.psum(mlp_parts[0].astype(jnp.bfloat16), "dp").astype(jnp.float32),
         lax.psum(mlp_parts[1].astype(jnp.bfloat16), "dp").astype(jnp.float32),

time: 828 us -> 778 us (0.940)
  waiting for transfers between devices: 384 us -> 328 us
  blocking collectives: 146 us -> 162 us
    reduce_scatter x1, waiting for transfers between devices: 87.4 us -> 0.01 us  [per_device(): lax.psum_scatter(up_weight_grad.astype(jnp.bfloat16), 'fsdp', scatter_dim...]
    reduce_scatter x1, waiting for transfers between devices: 0.01 us -> 75.2 us  [per_device(): lax.psum_scatter(qkv_weight_grad.astype(jnp.bfloat16), 'fsdp', scatter_di...]
    reduce_scatter x1, waiting for transfers between devices: 107 us -> 68.9 us  [per_device(): lax.psum_scatter(down_weight_grad.astype(jnp.bfloat16), 'fsdp', scatter_d...]
    all_gather x0 -> x1, blocking collectives: none -> 15.3 us  [per_device(): lax.all_gather(attn_parts[3].astype(jnp.bfloat16), 'dp')]
    psum x1, waiting for transfers between devices: 39.9 us -> 29.7 us  [per_device(): lax.psum(attn_parts[4].astype(jnp.bfloat16), 'dp').astype(jnp.float32)]
  transfers between devices with their start and end apart: 10 -> 10, of which waited for: 6 -> 6; matrix products, arithmetic and copies ran while one was open for 28% -> 30% of each run, Pallas kernels for 0% -> 0%
where the time goes in v1:
time: 778 us; the launch traced here: 773 us
  waiting for transfers between devices  328 us (42%)
  matrix products  191 us (25%)
  blocking collectives  162 us (21%)
  other arithmetic  48.4 us (6%)
  local copies, waits for them, and re-layouts  25.9 us (3%)
  between operations  17.4 us (2%)
    unnamed x2, blocking collectives  97.8 us
    reduce_scatter x1, waiting for transfers between devices, per_device(): lax.psum_scatter(qkv_weight_grad.astype(jnp.bfloat16), 'fsdp', scatter_di...  75.2 us
    reduce_scatter x1, waiting for transfers between devices, per_device(): lax.psum_scatter(down_weight_grad.astype(jnp.bfloat16), 'fsdp', scatter_d...  68.9 us
    all_gather x1, waiting for transfers between devices, per_device(): lax.all_gather(down_weight, 'fsdp', axis=0, tiled=True)  64.6 us
    reduce_scatter x1, waiting for transfers between devices, per_device(): lax.psum_scatter(time_weight_grad.astype(jnp.bfloat16), 'fsdp', scatter_d...  45.3 us
    all_gather x1, waiting for transfers between devices, per_device(): lax.all_gather(up_weight, 'fsdp', axis=0, tiled=True)  41.6 us
    dot_general x4, matrix products, rows_dot(): lax.dot_general(left, right, (((0,), (0,)), ((), ())), preferred_element_...  33.7 us
    psum x1, waiting for transfers between devices, per_device(): lax.psum(attn_parts[4].astype(jnp.bfloat16), 'dp').astype(jnp.float32)  29.7 us
  transfers between devices with their start and end apart: 10, of which 6 were waited for; matrix products, arithmetic and copies ran while one was open for 30% of the time, Pallas kernels for 0%

profile of v1, /device:TPU:0, one launch (start us, length us, event | category | flops | bytes accessed | tf_op | source)
XLA Modules:
  0.0 773.3 jit_solution(15781430290801108633)
XLA Ops:
  15.5 37.3 %all-reduce.12 = (bf16[1024]{0:T(1024)(128)(2,1)S(1)}, bf16[1024]{0:T(1024)(128)(2,1)S(1)}, bf16[1024]{0:T(1024)(128)(2,1)S(1)}, bf16[1024]{0:T(1024)(128)(2,1)S(1)}) all-reduce(bf16[1024]{0:T(1024)(128)(2,1)S(1)} %dynamic-update-slice.1, bf16[1024]{0:T(1024)(128)(2,1)S(1)} %dynamic-update-slice, ...), channel_id=1, replica_groups=mesh['dp'=2,'fsdp'=16] {'fsdp'}, use_global_device_ids=true, to_apply=%add.1 | all-reduce | flops 4096 | bytes 16384
  53.5 17.8 %all-gather.1 = bf16[16,1,256]{2,1,0:T(2,128)(2,1)S(1)} all-gather(bf16[1,1,256]{2,1,0:T(2,128)(2,1)S(1)} %reshape.824), channel_id=1, replica_groups=mesh['dp'=2,'fsdp'=16] {'fsdp'}, dimensions={0}, use_global_device_ids=true | all-gather | bytes 8704 | tf_op jit(solution)/shard_map/all_gather | solution.py:101
  72.9 21.8 %all_gather.47 = bf16[256,1024]{1,0:T(8,128)(2,1)S(1)} all-gather(bf16[16,1024]{1,0:T(8,128)(2,1)S(1)} %copy-done.12), channel_id=1, replica_groups=mesh['dp'=2,'fsdp'=16] {'fsdp'}, dimensions={0}, use_global_device_ids=true | all-gather | bytes 557056 | tf_op jit(solution)/shard_map/all_gather | solution.py:91
  94.9 8.6 %copy.59 = bf16[3072,1024]{1,0:T(8,128)(2,1)} copy(bf16[3072,1024]{0,1:T(8,128)(2,1)} %bitcast.285) | data formatting | bytes 12582912 | tf_op jit(solution)/shard_map/dot_general | solution.py:113
  103.5 6.4 convolution_bitcast_fusion.1
  114.1 32.2 %while.28 = (s32[]{:T(128)}, bf16[8,1,512,2,64]{2,4,3,1,0:T(8,128)(2,1)}, f32[8,1,2,512]{3,2,1,0:T(2,128)S(1)}, bf16[8,1,512,2,64]{2,4,3,1,0:T(8,128)(2,1)}, bf1...) while((s32[]{:T(128)}, ...), condition=%wide.region_5.6_spmd.clone, body=%wide.region_2.5_spmd.clone.sunk | while | flops 140574208 | bytes 6852709 | solution.py:143
  115.8 2.3 fusion.159
  136.0 2.3 fusion.159
  140.0 2.3 fusion.159
  144.0 2.3 fusion.159
  147.7 3.3 fusion.122
  151.3 41.6 %all-gather.11.cloned.1.call-done = bf16[1024,4096]{1,0:T(8,128)(2,1)} async-done(((bf16[64,4096]{1,0:T(8,128)(2,1)}), bf16[1024,4096]{1,0:T(8,128)(2,1)}) %all-gather.11.cloned.1.call-update) | async-done | bytes 8388624 | tf_op jit(solution)/shard_map/all_gather | solution.py:100
  192.9 10.3 %fusion.118 = f32[512,4096]{1,0:T(8,128)} fusion(bf16[1024,4096]{1,0:T(8,128)(2,1)} %all-gather.11.cloned.1.call-done, f32[1,512,1024]{2,1,0:T(8,128)S(1)} %get-tuple-element.270, f32[1024]{0:T(1024)S(1)} %convert_element_type.241, f32[1024]{0:T(1024)S(1)} %convert_element_type.240, f32[512]{0:T(512)S(1)} %add_rsqrt_fusion, ...), kind=kOutput, calls=%fused_computation.184 | convolution fusion | flops 4298113024 | bytes 18890752 | tf_op jit(solution)/shard_map/dot_general | solution.py:151
  203.2 64.6 %all-gather.13.cloned.1.call-done = bf16[4096,1024]{1,0:T(8,128)(2,1)} async-done(((bf16[256,1024]{1,0:T(8,128)(2,1)}), bf16[4096,1024]{1,0:T(8,128)(2,1)}) %all-gather.13.cloned.1.call-update) | async-done | bytes 8388624 | tf_op jit(solution)/shard_map/all_gather | solution.py:102
  267.9 13.6 %fusion.123 = (bf16[4096]{0:T(1024)(128)(2,1)S(1)}, bf16[512,4096]{1,0:T(8,128)(2,1)S(1)}) fusion(f32[512,4096]{1,0:T(8,128)} %fusion.118, f32[4096]{0:T(1024)S(1)} %bitcast.302, bf16[4096,1024]{1,0:T(8,128)(2,1)} %all-gather.13.cloned.1.call-done, f32[512]{0:T(512)S(1)} %fusion.109, bf16[1,512,1024]{2,1,0:T(8,128)(2,1)} %param.22), kind=kOutput, calls=%fused_computation.188 | convolution fusion | flops 4342673408 | bytes 22046720 | tf_op jit(solution)/shard_map/dot_general | solution.py:56
  281.5 5.2 fusion.79
  290.3 2.6 convolution_convert_fusion.4
  292.9 9.4 %convolution_convert_fusion.2 = bf16[1024,4096]{1,0:T(8,128)(2,1)} fusion(bf16[512,4096]{1,0:T(8,128)(2,1)} %copy-done.16, f32[1,512,1024]{2,1,0:T(8,128)S(1)} %get-tuple-element.270, f32[1024]{0:T(1024)S(1)} %convert_element_type.241, f32[1024]{0:T(1024)S(1)} %convert_element_type.240, f32[512]{0:T(512)S(1)} %add_rsqrt_fusion, ...), kind=kOutput, calls=%fused_computation.69 | convolution fusion | flops 4302307328 | bytes 14696448 | tf_op jit(solution)/shard_map/dot_general | solution.py:50
  302.5 4.6 convolution_convert_fusion.5
  309.3 13.6 %convolution_convert_fusion.1 = bf16[4096,1024]{1,0:T(8,128)(2,1)} fusion(bf16[1,512,1024]{2,1,0:T(8,128)(2,1)} %param.22, f32[512]{0:T(512)S(1)} %fusion.109, f32[512,4096]{1,0:T(8,128)} %fusion.118, f32[4096]{0:T(1024)S(1)} %bitcast.303), kind=kOutput, calls=%fused_computation.68 | convolution fusion | flops 4321705984 | bytes 17844224 | tf_op jit(solution)/shard_map/dot_general | solution.py:50
  323.0 83.2 %while.29 = (s32[]{:T(128)}, f32[8,1,512,2,64]{2,4,3,1,0:T(8,128)}, f32[8,1,512,2,64]{2,4,3,1,0:T(8,128)}, bf16[8,1,512,2,64]{2,4,3,1,0:T(8,128)(2,1)}, bf16[8,1...) while((s32[]{:T(128)}, f32[8,1,512,2,64]{2,4,3,1,0:T(8,128)}, ...), condition=%wide.region_12.13_spmd.clone, body=%wide.region_10.12_spmd.clone.sunk | while | flops 340393472 | bytes 17459324 | solution.py:222
  406.1 3.0 broadcast_multiply_fusion.1
  417.9 5.6 fusion.69
  424.4 8.1 %convolution_convert_fusion.3 = bf16[1024,3072]{1,0:T(8,128)(2,1)} fusion(bf16[512,3072]{0,1:T(8,128)(2,1)} %bitcast.295, bf16[1,512,1024]{2,1,0:T(8,128)(2,1)S(1)} %copy-done.2, f32[1024]{0:T(1024)S(1)} %broadcast_add_fusion, f32[1024]{0:T(1024)S(1)} %convert_element_type.235, f32[1024]{0:T(1024)S(1)} %convert_element_type.234, ...), kind=kOutput, calls=%fused_computation.70 | convolution fusion | flops 3228041216 | bytes 10502144 | tf_op jit(solution)/shard_map/dot_general | solution.py:50
  437.7 60.6 %all-reduce.11 = (bf16[1024]{0:T(1024)(128)(2,1)S(1)}, bf16[1024]{0:T(1024)(128)(2,1)S(1)}, bf16[1024]{0:T(1024)(128)(2,1)S(1)}, bf16[1024]{0:T(1024)(128)(2,1)S...) all-reduce(bf16[1024]{0:T(1024)(128)(2,1)S(1)} %dynamic-update-slic, ...), channel_id=1, replica_groups=mesh['dp'=2,'fsdp'=16] {'fsdp'}, use_global_device_ids=true, to_apply=%add.4 | all-reduce | flops 10240 | bytes 40960
  498.3 68.9 %reduce-scatter.14.cloned.1.call-done = bf16[256,1024]{1,0:T(8,128)(2,1)} async-done(((bf16[4096,1024]{1,0:T(8,128)(2,1)}), bf16[256,1024]{1,0:T(8,128)(2,1)}) %reduce-scatter.14.cloned.1.call-update) | async-done | bytes 524304 | tf_op jit(solution)/shard_map/reduce_scatter | solution.py:279
  567.2 12.4 %fusion.84 = bf16[1,512,1024]{2,1,0:T(8,128)(2,1)} fusion(f32[1,512,1024]{2,1,0:T(8,128)S(1)} %get-tuple-element.270, bf16[4096,1024]{1,0:T(8,128)(2,1)} %all-gather.13.cloned.1.call-done, f32[1024]{0:T(1024)S(1)} %convert_element_type.245, f32[512,4096]{1,0:T(8,128)} %fusion.118, f32[4096]{0:T(1024)S(1)} %bitcast.304), kind=kOutput, calls=%fused_computation.120 | convolution fusion | flops 4317511680 | bytes 19943424 | tf_op jit(solution)/shard_map/dot_general | solution.py:155
  581.8 45.3 %reduce-scatter.6.cloned.1.call-done = bf16[16,1024]{1,0:T(8,128)(2,1)} async-done(((bf16[256,1024]{1,0:T(8,128)(2,1)}), bf16[16,1024]{1,0:T(8,128)(2,1)}) %reduce-scatter.6.cloned.1.call-update) | async-done | bytes 32784 | tf_op jit(solution)/shard_map/reduce_scatter | solution.py:252
  627.1 9.1 %all-reduce.13 = (bf16[16,1024]{1,0:T(8,128)(2,1)S(1)}, bf16[64]{0:T(256)(128)(2,1)S(1)}, bf16[64]{0:T(256)(128)(2,1)S(1)}, bf16[64]{0:T(256)(128)(2,1)S(1)}, bf...) all-reduce(bf16[16,1024]{1,0:T(8,128)(2,1)} %reduce-scatter.6.clone, ...), channel_id=1, replica_groups=mesh['dp'=2,'fsdp'=16] {'dp'}, use_global_device_ids=true, to_apply=%region_18.19 | all-reduce | flops 16960 | bytes 67840 | tf_op jit(solution)/shard_map/psum | solution.py:289
  639.9 75.2 %reduce-scatter.8.cloned.1.call-done = bf16[64,3072]{1,0:T(8,128)(2,1)} async-done(((bf16[1024,3072]{1,0:T(8,128)(2,1)}), bf16[64,3072]{1,0:T(8,128)(2,1)}) %reduce-scatter.8.cloned.1.call-update) | async-done | bytes 393232 | tf_op jit(solution)/shard_map/reduce_scatter | solution.py:261
  715.1 15.3 %all-gather = bf16[128,3072]{1,0:T(8,128)(2,1)S(1)} all-gather(bf16[64,3072]{1,0:T(8,128)(2,1)} %reduce-scatter.8.cloned.1.call-done), channel_id=2, replica_groups=mesh['dp'=2,'fsdp'=16] {'dp'}, dimensions={0}, use_global_device_ids=true | all-gather | bytes 1179648 | tf_op jit(solution)/shard_map/all_gather | solution.py:292
  731.7 29.7 %all-reduce.17.cloned.1.call-done = (bf16[64,1024]{1,0:T(8,128)(2,1)}, bf16[64,4096]{1,0:T(8,128)(2,1)}, bf16[256,1024]{1,0:T(8,128)(2,1)}) async-done(((bf16[64,1024]{1,0:T(8,128)(2,1)}, bf16[64,4096]{1,0:T(8,128)(2,1)}, bf16[256,1024]{1,0:T(8,128)(2,1)}), (bf16[64,1024]{1,0:T(8,128)(2,1)}, bf16[64,4096]{1,0:T(8,128)(2,1)}, bf16[256,1024]{1,0:T(8,128)(2,1)})) %all-reduce.17.cloned.1.call-update) | async-done | bytes 1179664 | tf_op jit(solution)/shard_map/psum | solution.py:295
  (240 shorter events, 152.1 us)
Async XLA Ops:
  7.2 65.0 %copy-start.2 = (bf16[1,512,1024]{2,1,0:T(8,128)(2,1)S(1)}, bf16[1,512,1024]{2,1,0:T(8,128)(2,1)}, u32[]{:S(2)}) copy-start(bf16[1,512,1024]{2,1,0:T(8,128)(2,1)} %param.19) | copy-start | bytes 3145732
  7.2 65.7 %copy-start.12 = (bf16[16,1024]{1,0:T(8,128)(2,1)S(1)}, bf16[16,1024]{1,0:T(8,128)(2,1)}, u32[]{:S(2)}) copy-start(bf16[16,1024]{1,0:T(8,128)(2,1)} %param.23) | copy-start | bytes 98308
  7.2 87.7 %all-gather.7.cloned.1.call-start = ((), (), s32[]{:S(2)}) async-start(), calls=%async_computation.5 | async-start | bytes 6684672 | tf_op jit(solution)/shard_map/all_gather | solution.py:94
  7.9 138.5 %all-gather.9.cloned.1.call-start = ((), (), s32[]{:S(2)}) async-start(), calls=%async_computation.6 | async-start | bytes 2228224 | tf_op jit(solution)/shard_map/all_gather | solution.py:95
  8.7 86.0 %copy-start.13 = (bf16[1,256]{1,0:T(2,128)(2,1)S(1)}, bf16[1,256]{1,0:T(2,128)(2,1)}, u32[]{:S(2)}) copy-start(bf16[1,256]{1,0:T(2,128)(2,1)} %param.21) | copy-start | bytes 1540
  8.7 184.2 %all-gather.11.cloned.1.call-start = ((), (), s32[]{:S(2)}) async-start(), calls=%async_computation.7 | async-start | bytes 8912896 | tf_op jit(solution)/shard_map/all_gather | solution.py:100
  9.4 258.4 %all-gather.13.cloned.1.call-start = ((), (), s32[]{:S(2)}) async-start(), calls=%async_computation.8 | async-start | bytes 8912896 | tf_op jit(solution)/shard_map/all_gather | solution.py:102
  10.0 488.3 %reduce-scatter.10.cloned.1.call-start = ((), (), s32[]{:S(2)}) async-start(), calls=%async_computation.11 | async-start | bytes 2228224 | tf_op jit(solution)/shard_map/reduce_scatter | solution.py:264
  146.3 1.0 copy-start.6
  146.4 1.3 copy-start.7
  267.9 13.7 %copy-start.14 = (bf16[1024,4096]{1,0:T(8,128)(2,1)S(1)}, bf16[1024,4096]{1,0:T(8,128)(2,1)}, u32[]{:S(2)}) copy-start(bf16[1024,4096]{1,0:T(8,128)(2,1)} %all-gather.11.cloned.1.call-done) | copy-start | bytes 25165828
  281.5 5.2 copy-start.16
  286.7 1.2 copy-start.8
  288.0 2.3 copy-start.9
  288.9 1.3 copy-start.4
  292.9 205.4 %reduce-scatter.12.cloned.1.call-start = ((), (), s32[]{:S(2)}) async-start(), calls=%async_computation.12 | async-start | bytes 8912896 | tf_op jit(solution)/shard_map/reduce_scatter | solution.py:273
  302.3 264.8 %reduce-scatter.14.cloned.1.call-start = ((), (), s32[]{:S(2)}) async-start(), calls=%async_computation.13 | async-start | bytes 8912896 | tf_op jit(solution)/shard_map/reduce_scatter | solution.py:279
  322.9 304.2 %reduce-scatter.6.cloned.1.call-start = ((), (), s32[]{:S(2)}) async-start(), calls=%async_computation.9 | async-start | bytes 557056 | tf_op jit(solution)/shard_map/reduce_scatter | solution.py:252
  409.7 1.6 copy-start
  409.7 2.2 copy-start.1
  413.1 1.3 copy-start.10
  413.1 3.2 slice-start
  414.4 3.5 slice-start.1
  424.4 290.8 %reduce-scatter.8.cloned.1.call-start = ((), (), s32[]{:S(2)}) async-start(), calls=%async_computation.10 | async-start | bytes 6684672 | tf_op jit(solution)/shard_map/reduce_scatter | solution.py:261
  432.6 1.4 copy-start.15
  432.6 328.8 %all-reduce.17.cloned.1.call-start = ((), (), s32[]{:S(2)}) async-start(), calls=%async_computation.14 | async-start | bytes 2359296 | tf_op jit(solution)/shard_map/psum | solution.py:295
  567.2 12.8 %copy-start.3 = (f32[512,1024]{1,0:T(8,128)S(1)}, f32[512,1024]{1,0:T(8,128)}, u32[]{:S(2)}) copy-start(f32[512,1024]{1,0:T(8,128)} %get-tuple-element.272) | copy-start | bytes 6291460
  567.2 12.8 %copy-start.5 = (f32[1,512,1024]{2,1,0:T(8,128)S(1)}, f32[1,512,1024]{2,1,0:T(8,128)}, u32[]{:S(2)}) copy-start(f32[1,512,1024]{2,1,0:T(8,128)} %copy-done.4) | copy-start | bytes 6291460
  761.4 3.8 copy-start.11
Sparse Core Ops, SparseCore 0:
  10.3 64.5 all-gather.6
  77.0 40.6 all-gather.8
  119.9 73.0 all-gather.10
  195.0 72.8 all-gather.12
  293.0 60.3 reduce-scatter.9
  357.3 102.5 reduce-scatter.11
  464.0 103.0 reduce-scatter.13
  571.3 55.8 reduce-scatter.5
  631.0 84.0 reduce-scatter.7
  717.4 43.9 all-reduce.16
